TPU v7x, 32 devices: a whole 2x2x4 slice. The times are simulated.
32 devices in a mesh: groups: 2 (over y), expert: 8 (over z, core), section: 2 (over x), tensor: 1.
Axes of the slice: x: 2, y: 2, z: 4, core: 2. Of those that a mesh axis runs over, the one named last changes fastest.
Arguments:
- opening_residual: bfloat16 [2, 2048, 2048], P('section', ('groups', 'expert'), 'tensor'), parts along dimension 1, may hold values from -12 to 12
- incoming_residual: bfloat16 [1, 2048, 2048], P(None, ('groups', 'expert'), 'tensor'), parts along dimension 1, may hold values from -12 to 12
- stored_summaries: bfloat16 [2, 2, 16, 768, 512], P(None, 'section', ('groups', 'expert')), parts along dimension 2, may hold values from -40 to 40
- stored_counts: int32 [3, 16], P(None, ('groups', 'expert')), parts along dimension 1, may hold values from 1 to 768, as said below
- picked_specialists: int32 [2, 2, 2048, 6], P(None, 'section', ('groups', 'expert')), parts along dimension 2, may hold values from 0 to 15, all different within a row; in each aligned block of 128 rows (0 to 127, 128 to 255, ..., all dimensions but the last counted through in order) at most 64 rows name the same one
- chooser_mixing_share: float32 [2, 2, 2048, 6], P(None, 'section', ('groups', 'expert')), parts along dimension 2, may hold values from 0.05 to 0.4
- mixing_scale_factor: float32 [2, 2048], P('section'), may hold values from 0.25 to 1.75
- asking_projection: bfloat16 [2, 2048, 1024], P('section', None, 'tensor'), may hold values from -0.125 to 0.125
- summary_lookup_factor: bfloat16 [2, 8, 128, 512], P('section', 'tensor'), may hold values from -0.5 to 0.5
- summary_content_factor: bfloat16 [2, 8, 512, 128], P('section', 'tensor'), may hold values from -0.25 to 0.25
- merging_projection: bfloat16 [2, 1024, 2048], P('section', 'tensor'), may hold values from -0.1875 to 0.1875
- compress_projection: bfloat16 [2, 2048, 512], P('section', None, 'tensor'), may hold values from -0.125 to 0.125
- summary_scale_factor: float32 [2, 512], P('section'), may hold values from 0.25 to 1.75
- specialist_scale_factor: float32 [2, 2048], P('section', 'tensor'), may hold values from 0.25 to 1.75
- specialist_switch_factor: bfloat16 [2, 16, 2048, 704], P('section', 'expert', None, 'tensor'), may hold values from -0.125 to 0.125
- specialist_widen_factor: bfloat16 [2, 16, 2048, 704], P('section', 'expert', None, 'tensor'), may hold values from -0.125 to 0.125
- specialist_contract_factor: bfloat16 [2, 16, 704, 2048], P('section', 'expert', 'tensor'), may hold values from -0.21875 to 0.21875
Outputs:
- results: bfloat16 [2, 2, 2048, 2048], P(None, 'section', ('groups', 'expert'), 'tensor'), parts along dimension 2
There are 2 independent parts, one for each index of `groups`. A program takes and returns all parts, laid end to end along the dimension named above; an argument that names none is the same for every part. Nothing has to cross between parts.
Inputs may be any that keep to these rules, and one draw needn't show every extreme that they name: `picked_specialists`: in each aligned block of 128 rows (one sequence) no expert is chosen by more than 64 rows, a bound that some block reaches; each row names 6 different experts. `stored_counts`: in every microbatch some sequence has exactly 768 cached tokens.
All inputs are finite; a program needn't handle non-finite values.
Results may differ from a plain program's by a relative error of at most 0.04.
Values may be sent and summed in bfloat16 or wider, within the bound.
A program may use at most 128 MiB of HBM per device.

v0:
```python
import jax
import jax.numpy as jnp
from jax import lax
from jax.sharding import PartitionSpec as P

CAP = 64
RETURN_CHUNKS = 2
epsilon = 1e-06


def shifted(value, axis, steps):
    count = lax.axis_size(axis)
    initial, last = (max(0, -steps), min(count, count - steps))
    return lax.ppermute(value, axis, [(source, source + steps) for source in range(initial, last)])


def row_norm(values, gain_row):
    return (
        values * lax.rsqrt(jnp.mean(values * values, axis=-1, keepdims=True) + epsilon) * gain_row
    )


def attend(q_lat, cache_rows, new_rows, length, score_scale):
    piece_list = q_lat.shape[0]
    context = cache_rows.shape[0]
    key_rows = jnp.concatenate([cache_rows, new_rows], axis=0)
    scores = (
        jnp.einsum("thl,kl->thk", q_lat, key_rows, preferred_element_type=jnp.float32) * score_scale
    )
    position = lax.broadcasted_iota(jnp.int32, (piece_list, context + piece_list), 1)
    query_pos = lax.broadcasted_iota(jnp.int32, (piece_list, context + piece_list), 0)
    visible = jnp.where(position < context, position < length, position - context <= query_pos)
    scores = jnp.where(visible[:, None, :], scores, -jnp.inf)
    row_max = jnp.max(scores, axis=-1, keepdims=True)
    expd = jnp.where(visible[:, None, :], jnp.exp(scores - row_max), 0.0)
    attention = (expd / jnp.sum(expd, axis=-1, keepdims=True)).astype(jnp.bfloat16)
    return jnp.einsum(
        "thk,kl->thl", attention, key_rows, preferred_element_type=jnp.float32
    ).astype(jnp.bfloat16)


def shards(
    opening_residual,
    incoming_residual,
    stored_summaries,
    stored_counts,
    picked_specialists,
    chooser_mixing_share,
    mixing_scale_factor,
    asking_projection,
    summary_lookup_factor,
    summary_content_factor,
    merging_projection,
    compress_projection,
    summary_scale_factor,
    specialist_scale_factor,
    specialist_switch_factor,
    specialist_widen_factor,
    specialist_contract_factor,
):
    segment_ordinal = lax.axis_index("section")
    section_count = lax.axis_size("section")
    sources = lax.axis_size("expert")
    tick_count = stored_summaries.shape[0]
    piece_list = opening_residual.shape[1]
    inner_feature_midcount = opening_residual.shape[2]
    full_width = mixing_scale_factor.shape[1]
    local_heads = summary_lookup_factor.shape[1]
    head_size = summary_lookup_factor.shape[2]
    top_count = picked_specialists.shape[3]
    expert_local = specialist_switch_factor.shape[1]
    score_scale = head_size ** (-0.5)
    expert_ids = lax.broadcasted_iota(jnp.int32, (1, 1, 1, expert_local * sources), 3)
    shares_dense = jnp.sum(
        jnp.where(
            picked_specialists[:, 0][..., None] == expert_ids,
            chooser_mixing_share[:, 0][..., None],
            0.0,
        ),
        axis=2,
    )
    shares_all = lax.all_gather(jnp.swapaxes(shares_dense, 1, 2), "expert", axis=1, tiled=False)
    mine = lax.dynamic_slice_in_dim(
        shares_all, lax.axis_index("expert") * expert_local, expert_local, axis=2
    )
    chosen = mine > 0.0
    earlier_or_same = (
        lax.broadcasted_iota(jnp.int32, (piece_list, piece_list), 0)
        <= lax.broadcasted_iota(jnp.int32, (piece_list, piece_list), 1)
    ).astype(jnp.bfloat16)
    rank = jnp.einsum(
        "tjer,rq->tjeq",
        chosen.astype(jnp.bfloat16),
        earlier_or_same,
        preferred_element_type=jnp.float32,
    ).astype(jnp.int32)
    slots = lax.broadcasted_iota(jnp.int32, (1, 1, 1, CAP, 1), 3) + 1
    at_slot = (rank[..., None, :] == slots) & chosen[..., None, :]
    placed = at_slot.astype(jnp.bfloat16)
    slot_share = jnp.sum(jnp.where(at_slot, mine[..., None, :], 0.0), axis=-1)
    outputs = []
    present_carry = opening_residual[0]
    section_out = present_carry
    for step_index in range(tick_count):
        if step_index > 0:
            handed = shifted(section_out, "section", 1)
            present_carry = jnp.where(
                segment_ordinal == 0, incoming_residual[step_index - 1], handed
            )
        micro_index = step_index - segment_ordinal + section_count - 1
        length = lax.dynamic_index_in_dim(stored_counts[:, 0], micro_index, 0, keepdims=False)
        full_rows = lax.all_gather(present_carry, "tensor", axis=1, tiled=True)
        normed = row_norm(full_rows.astype(jnp.float32), mixing_scale_factor[0]).astype(
            jnp.bfloat16
        )
        queries = jnp.dot(normed, asking_projection[0], preferred_element_type=jnp.float32).astype(
            jnp.bfloat16
        )
        queries = queries.reshape(piece_list, local_heads, head_size)
        q_lat = jnp.einsum(
            "thd,hdl->thl", queries, summary_lookup_factor[0], preferred_element_type=jnp.float32
        ).astype(jnp.bfloat16)
        latent_part = jnp.dot(normed, compress_projection[0], preferred_element_type=jnp.float32)
        latent_raw = lax.all_gather(
            latent_part.astype(jnp.bfloat16), "tensor", axis=1, tiled=True
        ).astype(latent_part.dtype)
        new_latent = row_norm(latent_raw, summary_scale_factor[0]).astype(jnp.bfloat16)
        o_lat = attend(q_lat, stored_summaries[step_index, 0, 0], new_latent, length, score_scale)
        heads_out = jnp.einsum(
            "thl,hld->thd", o_lat, summary_content_factor[0], preferred_element_type=jnp.float32
        ).astype(jnp.bfloat16)
        heads_out = heads_out.reshape(piece_list, local_heads * head_size)
        head_terms = jnp.dot(heads_out, merging_projection[0], preferred_element_type=jnp.float32)
        residual = present_carry.astype(jnp.float32) + lax.psum_scatter(
            head_terms.astype(jnp.bfloat16), "tensor", scatter_dimension=1, tiled=True
        ).astype(jnp.float32)
        squares = lax.psum(jnp.sum(residual * residual, axis=1), "tensor")
        moe_input = (
            residual
            * lax.rsqrt(squares / full_width + epsilon)[:, None]
            * specialist_scale_factor[0]
        ).astype(jnp.bfloat16)
        whole_rows = lax.all_gather(moe_input, "tensor", axis=1, tiled=True)
        place = placed[step_index]
        share = slot_share[step_index]
        all_rows = lax.all_gather(whole_rows, "expert", axis=0, tiled=True)
        all_rows = all_rows.reshape(sources, piece_list, full_width)
        hidden_list = []
        for e in range(expert_local):
            rows_in = jnp.einsum(
                "jsr,jrd->jsd", place[:, e], all_rows, preferred_element_type=jnp.float32
            ).astype(jnp.bfloat16)
            rows_in = rows_in.reshape(sources * CAP, full_width)
            gate_values = jnp.dot(
                rows_in, specialist_switch_factor[0, e], preferred_element_type=jnp.float32
            )
            up_values = jnp.dot(
                rows_in, specialist_widen_factor[0, e], preferred_element_type=jnp.float32
            )
            hidden_list.append(
                (jax.nn.silu(gate_values) * up_values * share[:, e].reshape(-1, 1)).astype(
                    jnp.bfloat16
                )
            )
        chunk = full_width // RETURN_CHUNKS
        routed_list = []
        for c in range(RETURN_CHUNKS):
            total = None
            for e in range(expert_local):
                down = jnp.dot(
                    hidden_list[e],
                    specialist_contract_factor[0, e][:, c * chunk : (c + 1) * chunk],
                    preferred_element_type=jnp.float32,
                ).astype(jnp.bfloat16)
                term = jnp.einsum(
                    "jsr,jsd->jrd",
                    place[:, e],
                    down.reshape(sources, CAP, chunk),
                    preferred_element_type=jnp.float32,
                )
                total = term if total is None else total + term
            total = total.astype(jnp.bfloat16).reshape(sources * piece_list, chunk)
            routed_list.append(lax.psum_scatter(total, "expert", scatter_dimension=0, tiled=True))
        routed = jnp.concatenate(routed_list, axis=1)
        routed = lax.psum_scatter(routed, "tensor", scatter_dimension=1, tiled=True).astype(
            jnp.float32
        )
        section_out = (residual + routed).astype(jnp.bfloat16)
        outputs.append(section_out)
    return jnp.stack(outputs)[:, None]


def solution(mesh):
    in_specs = (
        P("section", ("groups", "expert"), "tensor"),
        P(None, ("groups", "expert"), "tensor"),
        P(None, "section", ("groups", "expert"), None, None),
        P(None, ("groups", "expert")),
        P(None, "section", ("groups", "expert"), None),
        P(None, "section", ("groups", "expert"), None),
        P("section", None),
        P("section", None, "tensor"),
        P("section", "tensor", None, None),
        P("section", "tensor", None, None),
        P("section", "tensor", None),
        P("section", None, "tensor"),
        P("section", None),
        P("section", "tensor"),
        P("section", "expert", None, "tensor"),
        P("section", "expert", None, "tensor"),
        P("section", "expert", "tensor", None),
    )
    out_specs = P(None, "section", ("groups", "expert"), "tensor")
    return jax.shard_map(shards, mesh=mesh, in_specs=in_specs, out_specs=out_specs, check_vma=False)
```

profile of v0, /device:TPU:0, one launch (start us, length us, event | category | flops | bytes accessed | tf_op | source)
XLA Modules:
  0.0 368.0 jit_solution(13593333180121278280)
XLA Ops:
  7.2 1.4 fusion.145
  8.6 2.2 multiply_reduce_fusion.3
  11.4 3.0 fusion.130
  14.4 1.3 slice_bitcast_fusion.2
  16.3 1.2 iota_compare_fusion.3
  17.5 1.0 multiply_convert_fusion.3
  18.5 1.5 fusion.159
  20.1 4.5 %fusion.105 = f32[128,8,896]{2,0,1:T(8,128)} fusion(bf16[1,8,128,512]{3,2,1,0:T(8,128)(2,1)S(1)} %copy-done.7, bf16[128,512]{1,0:T(8,128)(2,1)S(1)} %multiply_convert_fusion.3, bf16[768,512]{1,0:T(8,128)(2,1)} %get-tuple-element.10, bf16[16,8,8,128]{3,2,1,0:T(8,128)(2,1)S(1)} %fusion.130), kind=kOutput, calls=%fused_computation.97 | convolution fusion | flops 1076101120 | bytes 5898240 | tf_op jit(solution)/shard_map/thl,kl->thk/dot_general | solution.py:28
  24.6 6.7 %fusion.191 = (f32[128,8]{0,1:T(8,128)S(1)}, f32[128,8,896]{2,0,1:T(8,128)}) fusion(f32[128,8,896]{2,0,1:T(8,128)} %fusion.105, pred[128,896]{1,0:T(8,128)(4,1)} %get-tuple-element.20), kind=kOutput, calls=%fused_computation.204 | output fusion | flops 6423423 | bytes 7458816 | tf_op jit(solution)/shard_map/sub | solution.py:35
  31.3 3.9 %fusion.126 = bf16[8,128,128]{1,2,0:T(8,128)(2,1)S(1)} fusion(f32[128,8,896]{2,0,1:T(8,128)} %get-tuple-element.26, f32[128,8]{0,1:T(8,128)S(1)} %get-tuple-element.25, bf16[1,8,512,128]{3,2,1,0:T(8,128)(2,1)} %param.26, bf16[128,512]{1,0:T(8,128)(2,1)S(1)} %multiply_convert_fusion.3, bf16[768,512]{1,0:T(8,128)(2,1)S(1)} %copy-done.10), kind=kOutput, calls=%fused_computation.116 | convolution fusion | flops 1078067200 | bytes 5902336 | tf_op jit(solution)/shard_map/thl,hld->thd/dot_general | solution.py:129
  35.3 3.1 multiply_reduce_fusion.1
  39.6 16.3 %all-gather = f32[2,128,128]{2,1,0:T(8,128)S(1)} all-gather(f32[2,16,128]{2,1,0:T(8,128)S(1)} %bitcast.305), channel_id=2, replica_groups=mesh['groups'=2,'expert'=8,'section'=2,'tensor'=1] {'expert'}, dimensions={1}, use_global_device_ids=true | all-gather | bytes 147456 | tf_op jit(solution)/shard_map/all_gather | solution.py:82
  57.6 6.3 %slice_bitcast_fusion = (bf16[704,2048]{1,0:T(8,128)(2,1)}, bf16[704,2048]{1,0:T(8,128)(2,1)}) fusion(bf16[1,2,704,2048]{3,2,1,0:T(8,128)(2,1)} %param.33), kind=kLoop, calls=%fused_computation.40 | loop fusion | bytes 11534336 | tf_op jit(solution)/shard_map/squeeze | solution.py:172
  64.0 25.8 %all-gather.4.cloned.1.call-done = bf16[1024,2048]{1,0:T(8,128)(2,1)} async-done(((bf16[128,2048]{1,0:T(8,128)(2,1)}), bf16[1024,2048]{1,0:T(8,128)(2,1)}) %all-gather.4.cloned.1.call-update) | async-done | bytes 4194320 | tf_op jit(solution)/shard_map/all_gather | solution.py:146
  89.8 3.0 convolution_convert_fusion.2
  93.9 3.9 %fusion.16 = f32[512,704]{0,1:T(8,128)S(1)} fusion(bf16[512,2048]{1,0:T(8,128)(2,1)S(1)} %bitcast.286, bf16[1,2,2048,704]{2,3,1,0:T(8,128)(2,1)} %param.31), kind=kOutput, calls=%fused_computation.30 | convolution fusion | flops 1476395008 | bytes 6422528 | tf_op jit(solution)/shard_map/dot_general | solution.py:154
  97.9 1.7 fusion.24
  99.6 1.9 fusion.92
  101.5 1.0 convolution_convert_fusion.12
  103.3 1.9 fusion.98
  106.2 2.4 add_convert_fusion.3
  108.7 2.7 convolution_convert_fusion.9
  113.2 2.1 add_convert_fusion.2
  115.4 27.9 %reduce-scatter.5.cloned.1.call-done = bf16[128,1024]{1,0:T(8,128)(2,1)} async-done(((bf16[1024,1024]{1,0:T(8,128)(2,1)}), bf16[128,1024]{1,0:T(8,128)(2,1)}) %reduce-scatter.5.cloned.1.call-update) | async-done | bytes 262160 | tf_op jit(solution)/shard_map/reduce_scatter | solution.py:183
  143.3 36.7 %reduce-scatter.7.cloned.1.call-done = bf16[128,1024]{1,0:T(8,128)(2,1)} async-done(((bf16[1024,1024]{1,0:T(8,128)(2,1)}), bf16[128,1024]{1,0:T(8,128)(2,1)}) %reduce-scatter.7.cloned.1.call-update) | async-done | bytes 262160 | tf_op jit(solution)/shard_map/reduce_scatter | solution.py:183
  180.0 1.9 add_convert_fusion.5
  182.0 3.4 collective-permute-start
  185.4 8.5 %collective-permute-done = bf16[128,2048]{1,0:T(8,128)(2,1)S(1)} collective-permute-done((bf16[128,2048]{1,0:T(8,128)(2,1)}, bf16[128,2048]{1,0:T(8,128)(2,1)S(1)}, u32[]{:S(2)}, u32[]{:S(2)}) %collective-permute-start) | collective-permute-done | bytes 524320 | tf_op jit(solution)/shard_map/ppermute | solution.py:14
  193.9 1.3 fusion.148
  195.3 3.2 fusion.127
  199.7 4.5 %fusion.107 = f32[128,8,896]{2,0,1:T(8,128)} fusion(bf16[1,8,128,512]{3,2,1,0:T(8,128)(2,1)S(1)} %copy-done.8, bf16[128,512]{1,0:T(8,128)(2,1)S(1)} %multiply_convert_fusion.2, bf16[768,512]{1,0:T(8,128)(2,1)} %get-tuple-element.9, bf16[16,8,8,128]{3,2,1,0:T(8,128)(2,1)S(1)} %fusion.127), kind=kOutput, calls=%fused_computation.99 | convolution fusion | flops 1076101120 | bytes 5898240 | tf_op jit(solution)/shard_map/thl,kl->thk/dot_general | solution.py:28
  204.2 6.7 %fusion.192 = (f32[128,8]{0,1:T(8,128)S(1)}, f32[128,8,896]{2,0,1:T(8,128)}) fusion(f32[128,8,896]{2,0,1:T(8,128)} %fusion.107, pred[128,896]{1,0:T(8,128)(4,1)S(1)} %copy-done.18), kind=kOutput, calls=%fused_computation.205 | output fusion | flops 6423423 | bytes 7458816 | tf_op jit(solution)/shard_map/sub | solution.py:35
  211.0 3.7 %fusion.125 = bf16[8,128,128]{1,2,0:T(8,128)(2,1)S(1)} fusion(f32[128,8,896]{2,0,1:T(8,128)} %get-tuple-element.32, f32[128,8]{0,1:T(8,128)S(1)} %get-tuple-element.31, bf16[1,8,512,128]{3,2,1,0:T(8,128)(2,1)S(1)} %copy-done.28, bf16[128,512]{1,0:T(8,128)(2,1)S(1)} %multiply_convert_fusion.2, bf16[768,512]{1,0:T(8,128)(2,1)S(1)} %copy-done.9), kind=kOutput, calls=%fused_computation.115 | convolution fusion | flops 1078067200 | bytes 5902336 | tf_op jit(solution)/shard_map/thl,hld->thd/dot_general | solution.py:129
  214.7 3.0 multiply_reduce_fusion
  219.1 48.1 %all-gather.6.cloned.1.call-done = bf16[1024,2048]{1,0:T(8,128)(2,1)} async-done(((bf16[128,2048]{1,0:T(8,128)(2,1)}), bf16[1024,2048]{1,0:T(8,128)(2,1)}) %all-gather.6.cloned.1.call-update) | async-done | bytes 4194320 | tf_op jit(solution)/shard_map/all_gather | solution.py:146
  267.2 3.0 convolution_convert_fusion
  271.4 3.6 fusion.14
  275.1 1.9 fusion.101
  278.0 1.8 fusion.22
  279.8 1.9 fusion.95
  281.8 1.0 convolution_convert_fusion.7
  283.6 2.2 add_convert_fusion.1
  286.1 2.5 convolution_convert_fusion.4
  290.4 2.1 add_convert_fusion
  292.6 28.2 %reduce-scatter.9.cloned.1.call-done = bf16[128,1024]{1,0:T(8,128)(2,1)} async-done(((bf16[1024,1024]{1,0:T(8,128)(2,1)}), bf16[128,1024]{1,0:T(8,128)(2,1)}) %reduce-scatter.9.cloned.1.call-update) | async-done | bytes 262160 | tf_op jit(solution)/shard_map/reduce_scatter | solution.py:183
  320.8 36.9 %reduce-scatter.11.cloned.1.call-done = bf16[128,1024]{1,0:T(8,128)(2,1)} async-done(((bf16[1024,1024]{1,0:T(8,128)(2,1)}), bf16[128,1024]{1,0:T(8,128)(2,1)}) %reduce-scatter.11.cloned.1.call-update) | async-done | bytes 262160 | tf_op jit(solution)/shard_map/reduce_scatter | solution.py:183
  357.7 1.1 fusion.157
  358.8 2.1 maximum_bitcast_fusion
  (146 shorter events, 17.0 us)
Async XLA Ops:
  6.5 2.0 copy-start
  6.5 4.8 %copy-start.4 = (bf16[1,128,2048]{2,1,0:T(8,128)(2,1)S(1)}, bf16[1,128,2048]{2,1,0:T(8,128)(2,1)}, u32[]{:S(2)}) copy-start(bf16[1,128,2048]{2,1,0:T(8,128)(2,1)} %param.17) | copy-start | bytes 1572868
  6.5 4.8 %copy-start.19 = (f32[1,2048]{1,0:T(1,128)S(1)}, f32[1,2048]{1,0:T(1,128)}, u32[]{:S(2)}) copy-start(f32[1,2048]{1,0:T(1,128)} %param.23) | copy-start | bytes 24580
  6.5 83.2 %all-gather.4.cloned.1.call-start = ((), (), s32[]{:S(2)}) async-start(), calls=%async_computation.4 | async-start | bytes 4718592 | tf_op jit(solution)/shard_map/all_gather | solution.py:146
  10.8 3.5 copy-start.17
  11.3 4.3 %copy-start.27 = (s32[3,1]{0,1:T(1,128)S(1)}, s32[3,1]{0,1:T(1,128)}, u32[]{:S(2)}) copy-start(s32[3,1]{0,1:T(1,128)} %param.20) | copy-start | bytes 40
  11.3 6.1 %copy-start.23 = (f32[1,512]{1,0:T(1,128)S(1)}, f32[1,512]{1,0:T(1,128)}, u32[]{:S(2)}) copy-start(f32[1,512]{1,0:T(1,128)} %param.29) | copy-start | bytes 6148
  14.3 5.7 %copy-start.7 = (bf16[1,8,128,512]{3,2,1,0:T(8,128)(2,1)S(1)}, bf16[1,8,128,512]{3,2,1,0:T(8,128)(2,1)}, u32[]{:S(2)}) copy-start(bf16[1,8,128,512]{3,2,1,0:T(8,128)(2,1)} %param.25) | copy-start | bytes 3145732
  24.6 6.7 %copy-start.10 = (bf16[768,512]{1,0:T(8,128)(2,1)S(1)}, bf16[768,512]{1,0:T(8,128)(2,1)}, u32[]{:S(2)}) copy-start(bf16[768,512]{1,0:T(8,128)(2,1)} %get-tuple-element.10) | copy-start | bytes 2359300
  35.3 3.2 copy-start.20
  35.3 4.2 %copy-start.25 = (s32[2,1,128,6]{2,1,3,0:T(1,128)S(1)}, s32[2,1,128,6]{2,1,3,0:T(1,128)}, u32[]{:S(2)}) copy-start(s32[2,1,128,6]{2,1,3,0:T(1,128)} %param.21) | copy-start | bytes 18436
  35.3 4.2 %copy-start.26 = (f32[2,1,128,6]{2,1,3,0:T(1,128)S(1)}, f32[2,1,128,6]{2,1,3,0:T(1,128)}, u32[]{:S(2)}) copy-start(f32[2,1,128,6]{2,1,3,0:T(1,128)} %param.22) | copy-start | bytes 18436
  39.5 103.8 %reduce-scatter.5.cloned.1.call-start = ((), (), s32[]{:S(2)}) async-start(), calls=%async_computation.5 | async-start | bytes 2359296 | tf_op jit(solution)/shard_map/reduce_scatter | solution.py:183
  89.8 3.4 copy-start.2
  93.2 4.6 %slice-start = ((s8[5767168]{0:T(1024)(128)(4,1)}), s8[4194304]{0:T(1024)(128)(4,1)S(1)}, s32[]{:S(2)}) async-start(s8[5767168]{0:T(1024)(128)(4,1)} %bitcast.316), calls=%async_computation.10 | async-start | bytes 8388608
  93.9 3.9 %slice-start.1 = ((s8[5767168]{0:T(1024)(128)(4,1)}), s8[1572864]{0:T(1024)(128)(4,1)S(1)}, s32[]{:S(2)}) async-start(s8[5767168]{0:T(1024)(128)(4,1)} %bitcast.316), calls=%async_computation.11 | async-start | bytes 3145728
  93.9 5.6 %slice-start.4 = ((s8[5767168]{0:T(1024)(128)(4,1)}), s8[4194304]{0:T(1024)(128)(4,1)S(1)}, s32[]{:S(2)}) async-start(s8[5767168]{0:T(1024)(128)(4,1)} %bitcast.320), calls=%async_computation.14 | async-start | bytes 8388608
  97.8 1.7 slice-start.5
  99.6 1.9 copy-start.11
  101.5 1.0 copy-start.29
  103.3 1.9 copy-start.15
  108.6 71.4 %reduce-scatter.7.cloned.1.call-start = ((), (), s32[]{:S(2)}) async-start(), calls=%async_computation.6 | async-start | bytes 2359296 | tf_op jit(solution)/shard_map/reduce_scatter | solution.py:183
  108.6 2.8 copy-start.12
  108.6 2.8 copy-start.30
  115.3 151.9 %all-gather.6.cloned.1.call-start = ((), (), s32[]{:S(2)}) async-start(), calls=%async_computation.7 | async-start | bytes 4718592 | tf_op jit(solution)/shard_map/all_gather | solution.py:146
  182.0 12.0 %collective-permute-start = (bf16[128,2048]{1,0:T(8,128)(2,1)}, bf16[128,2048]{1,0:T(8,128)(2,1)S(1)}, u32[]{:S(2)}, u32[]{:S(2)}) collective-permute-start(bf16[128,2048]{1,0:T(8,128)(2,1)} %add_convert_fusion.5), channel_id=1, source_target_pairs={{0,1},{2,3},{4,5},{6,7},{8,9},{10,11},{12,13},{14,15},{16,17},{18,... | collective-permute-start | bytes 1572872 | tf_op jit(solution)/shard_map/ppermute | solution.py:14
  195.2 3.8 %copy-start.5 = (bf16[128,2048]{1,0:T(8,128)(2,1)}, bf16[128,2048]{1,0:T(8,128)(2,1)S(1)}, u32[]{:S(2)}) copy-start(bf16[128,2048]{1,0:T(8,128)(2,1)S(1)} %get-tuple-element.6) | copy-start | bytes 1572868
  195.3 3.8 %copy-start.24 = (f32[1,512]{1,0:T(1,128)S(1)}, f32[1,512]{1,0:T(1,128)}, u32[]{:S(2)}) copy-start(f32[1,512]{1,0:T(1,128)} %param.29) | copy-start | bytes 6148
  198.4 1.2 copy-start.8
  199.7 4.5 %copy-start.18 = (pred[128,896]{1,0:T(8,128)(4,1)S(1)}, pred[128,896]{1,0:T(8,128)(4,1)}, u32[]{:S(2)}) copy-start(pred[128,896]{1,0:T(8,128)(4,1)} %get-tuple-element.19) | copy-start | bytes 344068
  204.2 6.8 %copy-start.9 = (bf16[768,512]{1,0:T(8,128)(2,1)S(1)}, bf16[768,512]{1,0:T(8,128)(2,1)}, u32[]{:S(2)}) copy-start(bf16[768,512]{1,0:T(8,128)(2,1)} %get-tuple-element.9) | copy-start | bytes 2359300
  204.2 6.8 %copy-start.28 = (bf16[1,8,512,128]{3,2,1,0:T(8,128)(2,1)S(1)}, bf16[1,8,512,128]{3,2,1,0:T(8,128)(2,1)}, u32[]{:S(2)}) copy-start(bf16[1,8,512,128]{3,2,1,0:T(8,128)(2,1)} %param.26) | copy-start | bytes 3145732
  210.9 3.7 %copy-start.6 = (bf16[128,2048]{1,0:T(8,128)(2,1)S(1)}, bf16[128,2048]{1,0:T(8,128)(2,1)}, u32[]{:S(2)}) copy-start(bf16[128,2048]{1,0:T(8,128)(2,1)} %copy-done.5) | copy-start | bytes 1572868
  214.7 4.3 %copy-start.22 = (f32[8,1,64]{2,0,1:T(8,128)S(1)}, f32[8,1,64]{2,0,1:T(8,128)}, u32[]{:S(2)}) copy-start(f32[8,1,64]{2,0,1:T(8,128)} %get-tuple-element.15) | copy-start | bytes 6148
  214.7 4.4 %copy-start.21 = (f32[8,1,64]{2,0,1:T(8,128)S(1)}, f32[8,1,64]{2,0,1:T(8,128)}, u32[]{:S(2)}) copy-start(f32[8,1,64]{2,0,1:T(8,128)} %get-tuple-element.16) | copy-start | bytes 6148
  218.7 102.1 %reduce-scatter.9.cloned.1.call-start = ((), (), s32[]{:S(2)}) async-start(), calls=%async_computation.8 | async-start | bytes 2359296 | tf_op jit(solution)/shard_map/reduce_scatter | solution.py:183
  267.2 3.4 copy-start.3
  267.2 7.8 %slice-start.6 = ((s8[5767168]{0:T(1024)(128)(4,1)}), s8[4194304]{0:T(1024)(128)(4,1)S(1)}, s32[]{:S(2)}) async-start(s8[5767168]{0:T(1024)(128)(4,1)} %bitcast.322), calls=%async_computation.16 | async-start | bytes 8388608
  270.7 4.4 %slice-start.7 = ((s8[5767168]{0:T(1024)(128)(4,1)}), s8[1572864]{0:T(1024)(128)(4,1)S(1)}, s32[]{:S(2)}) async-start(s8[5767168]{0:T(1024)(128)(4,1)} %bitcast.322), calls=%async_computation.17 | async-start | bytes 3145728
  271.4 6.6 %slice-start.2 = ((s8[5767168]{0:T(1024)(128)(4,1)}), s8[4194304]{0:T(1024)(128)(4,1)S(1)}, s32[]{:S(2)}) async-start(s8[5767168]{0:T(1024)(128)(4,1)} %bitcast.318), calls=%async_computation.12 | async-start | bytes 8388608
  275.1 1.9 copy-start.16
  275.1 2.9 slice-start.3
  279.8 2.0 copy-start.13
  283.6 2.5 copy-start.32
  285.8 71.9 %reduce-scatter.11.cloned.1.call-start = ((), (), s32[]{:S(2)}) async-start(), calls=%async_computation.9 | async-start | bytes 2359296 | tf_op jit(solution)/shard_map/reduce_scatter | solution.py:183
  286.1 2.5 copy-start.14
  286.1 2.5 copy-start.34
  292.5 68.4 %copy-start.1 = (bf16[1,2048,512]{2,1,0:T(8,128)(2,1)S(1)}, bf16[1,2048,512]{2,1,0:T(8,128)(2,1)}, u32[]{:S(2)}) copy-start(bf16[1,2048,512]{2,1,0:T(8,128)(2,1)} %param.28) | copy-start | bytes 6291460
  (3 other events, 3.1 us)
Sparse Core Ops, SparseCore 0:
  39.6 50.1 all-gather.3
  108.7 34.5 reduce-scatter.4
  145.6 34.3 reduce-scatter.6
  218.8 48.3 all-gather.5
  285.9 34.8 reduce-scatter.8
  323.0 34.6 reduce-scatter.10
where the time goes:
time: 374 us; the launch traced here: 368 us
  waiting for transfers between devices  212 us (57%)
  matrix products  81 us (22%)
  other arithmetic  29.1 us (8%)
  blocking collectives  16.3 us (4%)
  between operations  14.6 us (4%)
  local copies, waits for them, and re-layouts  10.7 us (3%)
  starting transfers between devices  4.1 us (1%)
    reduce_scatter x4, waiting for transfers between devices, shards(): lax.psum_scatter(total, 'expert', scatter_dimension=0, tiled=True)  130 us
    all_gather x2, waiting for transfers between devices, shards(): all_rows = lax.all_gather(whole_rows, 'expert', axis=0, tiled=True)  73.9 us
    all_gather x1, blocking collectives, shards(): lax.all_gather(jnp.swapaxes(shares_dense, 1, 2), 'expert', axis=1, tiled=...  16.3 us
    sub x2, other arithmetic, attend(): expd = jnp.where(visible[:, None, :], jnp.exp(scores - row_max), 0.0)  13.5 us
    dot_general x8, matrix products, shards(): jnp.einsum('jsr,jsd->jrd', place[:, e], down.reshape(sources, CAP, chunk)...  11.8 us
    dot_general x8, matrix products, shards(): jnp.dot(hidden_list[e], specialist_contract_factor[0, e][:, c * chunk:(c...  11.2 us
    dot_general x4, matrix products, shards(): jnp.dot(rows_in, specialist_switch_factor[0, e], preferred_element_type=j...  10.9 us
    dot_general x2, matrix products, attend(): jnp.einsum('thl,kl->thk', q_lat, key_rows, preferred_element_type=jnp.flo...  9.03 us
  transfers between devices with their start and end apart: 7, of which 7 were waited for; matrix products, arithmetic and copies ran while one was open for 6% of the time, Pallas kernels for 0%

commit v1 on v0

--- a/solution.py
+++ b/solution.py
@@ -143,7 +143,14 @@
         whole_rows = lax.all_gather(moe_input, "tensor", axis=1, tiled=True)
         place = placed[step_index]
         share = slot_share[step_index]
-        all_rows = lax.all_gather(whole_rows, "expert", axis=0, tiled=True)
+        peers = lax.axis_size("expert")
+        right = [(i, (i + 1) % peers) for i in range(peers)]
+        parts = [whole_rows]
+        for far in range(1, peers):
+            parts = [lax.ppermute(parts[0], "expert", right), *parts]
+        full = jnp.concatenate(parts, axis=0)
+        shift = (lax.axis_index("expert") + 1) * parts[-1].shape[0]
+        all_rows = jnp.roll(full, shift, axis=0)
         all_rows = all_rows.reshape(sources, piece_list, full_width)
         hidden_list = []
         for e in range(expert_local):

time: 374 us -> 449 us (1.20)
  waiting for transfers between devices: 212 us -> 270 us
  starting transfers between devices: 4.1 us -> 14.6 us
  matrix products: 81 us -> 71.2 us
  other arithmetic: 29.1 us -> 36.9 us
  local copies, waits for them, and re-layouts: 10.7 us -> 17.3 us
    ppermute x0 -> x14, waiting for transfers between devices: none -> 131 us  [shards(): parts = [lax.ppermute(parts[0], 'expert', right), *parts]]
    all_gather x2 -> x0, waiting for transfers between devices: 73.9 us -> none  [shards(): all_rows = lax.all_gather(whole_rows, 'expert', axis=0, tiled=True)]
    ppermute x0 -> x14, starting transfers between devices: none -> 10.4 us  [shards(): parts = [lax.ppermute(parts[0], 'expert', right), *parts]]
    concatenate x0 -> x4, other arithmetic: none -> 9.33 us  [the longest x2 9.02 us: shards(): all_rows = jnp.roll(full, shift, axis=0)]
    unnamed x91 -> x111, local copies, waits for them, and re-layouts: 1.52 us -> 10.8 us
    dot_general x4, matrix products: 7.47 us -> 2.82 us  [shards(): jnp.einsum('jsr,jrd->jsd', place[:, e], all_rows, preferred_element_type=...]
  transfers between devices with their start and end apart: 7 -> 19, of which waited for: 7 -> 18; matrix products, arithmetic and copies ran while one was open for 6% -> 4% of each run, Pallas kernels for 0% -> 0%
where the time goes in v1:
time: 449 us; the launch traced here: 442 us
  waiting for transfers between devices  270 us (60%)
  matrix products  71.2 us (16%)
  other arithmetic  36.9 us (8%)
  local copies, waits for them, and re-layouts  17.3 us (4%)
  blocking collectives  17.1 us (4%)
  starting transfers between devices  14.6 us (3%)
  between operations  14.4 us (3%)
    ppermute x14, waiting for transfers between devices, shards(): parts = [lax.ppermute(parts[0], 'expert', right), *parts]  131 us
    reduce_scatter x4, waiting for transfers between devices, shards(): lax.psum_scatter(total, 'expert', scatter_dimension=0, tiled=True)  130 us
    all_gather x1, blocking collectives, shards(): lax.all_gather(jnp.swapaxes(shares_dense, 1, 2), 'expert', axis=1, tiled=...  17.1 us
    sub x2, other arithmetic, attend(): expd = jnp.where(visible[:, None, :], jnp.exp(scores - row_max), 0.0)  13.5 us
    dot_general x8, matrix products, shards(): jnp.einsum('jsr,jsd->jrd', place[:, e], down.reshape(sources, CAP, chunk)...  11.5 us
    dot_general x8, matrix products, shards(): jnp.dot(hidden_list[e], specialist_contract_factor[0, e][:, c * chunk:(c...  11.3 us
    unnamed x111, local copies, waits for them, and re-layouts  10.8 us
    ppermute x14, starting transfers between devices, shards(): parts = [lax.ppermute(parts[0], 'expert', right), *parts]  10.4 us
  transfers between devices with their start and end apart: 19, of which 18 were waited for; matrix products, arithmetic and copies ran while one was open for 4% of the time, Pallas kernels for 0%

profile of v1, /device:TPU:0, one launch (start us, length us, event | category | flops | bytes accessed | tf_op | source)
XLA Modules:
  0.0 441.5 jit_solution(5746782567546266638)
XLA Ops:
  8.6 3.2 fusion.132
  19.4 4.5 %fusion.107 = f32[128,8,896]{2,0,1:T(8,128)} fusion(bf16[1,8,128,512]{3,2,1,0:T(8,128)(2,1)S(1)} %copy-done.5, bf16[128,512]{1,0:T(8,128)(2,1)S(1)} %multiply_convert_fusion.3, bf16[768,512]{1,0:T(8,128)(2,1)} %get-tuple-element.11, bf16[16,8,8,128]{3,2,1,0:T(8,128)(2,1)S(1)} %fusion.132), kind=kOutput, calls=%fused_computation.103 | convolution fusion | flops 1076101120 | bytes 5898240 | tf_op jit(solution)/shard_map/thl,kl->thk/dot_general | solution.py:28
  23.9 6.8 %fusion.193 = (f32[128,8]{0,1:T(8,128)S(1)}, f32[128,8,896]{2,0,1:T(8,128)}) fusion(f32[128,8,896]{2,0,1:T(8,128)} %fusion.107, pred[128,896]{1,0:T(8,128)(4,1)} %get-tuple-element.21), kind=kOutput, calls=%fused_computation.226 | output fusion | flops 6423423 | bytes 7458816 | tf_op jit(solution)/shard_map/sub | solution.py:35
  30.6 3.9 fusion.128
  34.6 3.1 multiply_reduce_fusion.1
  38.5 10.9 %collective-permute-done = bf16[128,2048]{1,0:T(8,128)(2,1)S(1)} collective-permute-done((bf16[128,2048]{1,0:T(8,128)(2,1)S(1)}, bf16[128,2048]{1,0:T(8,128)(2,1)S(1)}, u32[]{:S(2)}, u32[]{:S(2)}) %collective-permute-start) | collective-permute-done | bytes 524320 | tf_op jit(solution)/shard_map/ppermute | solution.py:150
  50.2 10.4 %collective-permute-done.1 = bf16[128,2048]{1,0:T(8,128)(2,1)S(1)} collective-permute-done((bf16[128,2048]{1,0:T(8,128)(2,1)S(1)}, bf16[128,2048]{1,0:T(8,128)(2,1)S(1)}, u32[]{:S(2)}, u32[]{:S(2)}) %collective-permute-start.1) | collective-permute-done | bytes 524320 | tf_op jit(solution)/shard_map/ppermute | solution.py:150
  61.4 10.5 %collective-permute-done.2 = bf16[128,2048]{1,0:T(8,128)(2,1)} collective-permute-done((bf16[128,2048]{1,0:T(8,128)(2,1)S(1)}, bf16[128,2048]{1,0:T(8,128)(2,1)}, u32[]{:S(2)}, u32[]{:S(2)}) %collective-permute-start.2) | collective-permute-done | bytes 524320 | tf_op jit(solution)/shard_map/ppermute | solution.py:150
  72.0 17.1 %all-gather = f32[2,128,128]{2,1,0:T(8,128)S(1)} all-gather(f32[2,16,128]{2,1,0:T(8,128)S(1)} %bitcast.309), channel_id=2, replica_groups=mesh['groups'=2,'expert'=8,'section'=2,'tensor'=1] {'expert'}, dimensions={1}, use_global_device_ids=true | all-gather | bytes 147456 | tf_op jit(solution)/shard_map/all_gather | solution.py:82
  90.0 9.9 %collective-permute-done.4 = bf16[128,2048]{1,0:T(8,128)(2,1)} collective-permute-done((bf16[128,2048]{1,0:T(8,128)(2,1)}, bf16[128,2048]{1,0:T(8,128)(2,1)}, u32[]{:S(2)}, u32[]{:S(2)}) %collective-permute-start.4) | collective-permute-done | bytes 524320 | tf_op jit(solution)/shard_map/ppermute | solution.py:150
  101.0 9.7 %collective-permute-done.5 = bf16[128,2048]{1,0:T(8,128)(2,1)} collective-permute-done((bf16[128,2048]{1,0:T(8,128)(2,1)}, bf16[128,2048]{1,0:T(8,128)(2,1)}, u32[]{:S(2)}, u32[]{:S(2)}) %collective-permute-start.5) | collective-permute-done | bytes 524320 | tf_op jit(solution)/shard_map/ppermute | solution.py:150
  110.7 9.6 %collective-permute-start.6 = (bf16[128,2048]{1,0:T(8,128)(2,1)}, bf16[128,2048]{1,0:T(8,128)(2,1)S(1)}, u32[]{:S(2)}, u32[]{:S(2)}) collective-permute-start(bf16[128,2048]{1,0:T(8,128)(2,1)} %collective-permute-done.5), channel_id=1, source_target_pairs={{0,2},{2,4},{4,6},{6,8},{8,10},{10,12},{12,14},{14,0},{1,3},{3,5},... | collective-permute-start | bytes 1572872 | tf_op jit(solution)/shard_map/ppermute | solution.py:150
  120.3 3.7 slice_bitcast_fusion
  124.0 6.9 %collective-permute-done.6 = bf16[128,2048]{1,0:T(8,128)(2,1)S(1)} collective-permute-done((bf16[128,2048]{1,0:T(8,128)(2,1)}, bf16[128,2048]{1,0:T(8,128)(2,1)S(1)}, u32[]{:S(2)}, u32[]{:S(2)}) %collective-permute-start.6) | collective-permute-done | bytes 524320 | tf_op jit(solution)/shard_map/ppermute | solution.py:150
  135.5 4.4 %fusion.3 = bf16[1024,2048]{1,0:T(8,128)(2,1)S(1)} fusion(s32[]{:T(128)S(6)} %select_n.80, bf16[1024,2048]{1,0:T(8,128)(2,1)S(1)} %constant_dynamic-update-slice_fusion), kind=kLoop, calls=%fused_computation.7 | loop fusion | flops 8388608 | bytes 8388612 | tf_op jit(solution)/shard_map/jit(_roll_dynamic)/concatenate | solution.py:153
  143.1 1.7 fusion.26
  144.9 1.9 fusion.94
  148.6 1.9 fusion.100
  151.6 2.1 add_convert_fusion.3
  154.2 2.7 convolution_convert_fusion.9
  158.8 2.1 add_convert_fusion.2
  161.0 27.7 %reduce-scatter.5.cloned.1.call-done = bf16[128,1024]{1,0:T(8,128)(2,1)} async-done(((bf16[1024,1024]{1,0:T(8,128)(2,1)}), bf16[128,1024]{1,0:T(8,128)(2,1)}) %reduce-scatter.5.cloned.1.call-update) | async-done | bytes 262160 | tf_op jit(solution)/shard_map/reduce_scatter | solution.py:190
  188.6 37.0 %reduce-scatter.7.cloned.1.call-done = bf16[128,1024]{1,0:T(8,128)(2,1)} async-done(((bf16[1024,1024]{1,0:T(8,128)(2,1)}), bf16[128,1024]{1,0:T(8,128)(2,1)}) %reduce-scatter.7.cloned.1.call-update) | async-done | bytes 262160 | tf_op jit(solution)/shard_map/reduce_scatter | solution.py:190
  225.6 2.0 add_convert_fusion.5
  227.6 3.4 collective-permute-start.7
  231.1 8.7 %collective-permute-done.7 = bf16[128,2048]{1,0:T(8,128)(2,1)S(1)} collective-permute-done((bf16[128,2048]{1,0:T(8,128)(2,1)}, bf16[128,2048]{1,0:T(8,128)(2,1)S(1)}, u32[]{:S(2)}, u32[]{:S(2)}) %collective-permute-start.7) | collective-permute-done | bytes 524320 | tf_op jit(solution)/shard_map/ppermute | solution.py:14
  241.1 3.2 fusion.129
  245.0 4.5 %fusion.109 = f32[128,8,896]{2,0,1:T(8,128)} fusion(bf16[1,8,128,512]{3,2,1,0:T(8,128)(2,1)S(1)} %copy-done.6, bf16[128,512]{1,0:T(8,128)(2,1)S(1)} %multiply_convert_fusion.2, bf16[768,512]{1,0:T(8,128)(2,1)} %get-tuple-element.10, bf16[16,8,8,128]{3,2,1,0:T(8,128)(2,1)S(1)} %fusion.129), kind=kOutput, calls=%fused_computation.105 | convolution fusion | flops 1076101120 | bytes 5898240 | tf_op jit(solution)/shard_map/thl,kl->thk/dot_general | solution.py:28
  249.5 6.7 %fusion.194 = (f32[128,8]{0,1:T(8,128)S(1)}, f32[128,8,896]{2,0,1:T(8,128)}) fusion(f32[128,8,896]{2,0,1:T(8,128)} %fusion.109, pred[128,896]{1,0:T(8,128)(4,1)S(1)} %copy-done.22), kind=kOutput, calls=%fused_computation.227 | output fusion | flops 6423423 | bytes 7458816 | tf_op jit(solution)/shard_map/sub | solution.py:35
  256.2 3.7 fusion.127
  260.0 3.0 multiply_reduce_fusion
  263.3 10.4 %collective-permute-done.8 = bf16[128,2048]{1,0:T(8,128)(2,1)S(1)} collective-permute-done((bf16[128,2048]{1,0:T(8,128)(2,1)S(1)}, bf16[128,2048]{1,0:T(8,128)(2,1)S(1)}, u32[]{:S(2)}, u32[]{:S(2)}) %collective-permute-start.8) | collective-permute-done | bytes 524320 | tf_op jit(solution)/shard_map/ppermute | solution.py:150
  273.6 10.4 %collective-permute-done.9 = bf16[128,2048]{1,0:T(8,128)(2,1)S(1)} collective-permute-done((bf16[128,2048]{1,0:T(8,128)(2,1)S(1)}, bf16[128,2048]{1,0:T(8,128)(2,1)S(1)}, u32[]{:S(2)}, u32[]{:S(2)}) %collective-permute-start.9) | collective-permute-done | bytes 524320 | tf_op jit(solution)/shard_map/ppermute | solution.py:150
  284.1 10.4 %collective-permute-done.10 = bf16[128,2048]{1,0:T(8,128)(2,1)S(1)} collective-permute-done((bf16[128,2048]{1,0:T(8,128)(2,1)S(1)}, bf16[128,2048]{1,0:T(8,128)(2,1)S(1)}, u32[]{:S(2)}, u32[]{:S(2)}) %collective-permute-start.10) | collective-permute-done | bytes 524320 | tf_op jit(solution)/shard_map/ppermute | solution.py:150
  294.5 10.4 %collective-permute-done.11 = bf16[128,2048]{1,0:T(8,128)(2,1)S(1)} collective-permute-done((bf16[128,2048]{1,0:T(8,128)(2,1)S(1)}, bf16[128,2048]{1,0:T(8,128)(2,1)S(1)}, u32[]{:S(2)}, u32[]{:S(2)}) %collective-permute-start.11) | collective-permute-done | bytes 524320 | tf_op jit(solution)/shard_map/ppermute | solution.py:150
  304.9 10.4 %collective-permute-done.12 = bf16[128,2048]{1,0:T(8,128)(2,1)S(1)} collective-permute-done((bf16[128,2048]{1,0:T(8,128)(2,1)S(1)}, bf16[128,2048]{1,0:T(8,128)(2,1)S(1)}, u32[]{:S(2)}, u32[]{:S(2)}) %collective-permute-start.12) | collective-permute-done | bytes 524320 | tf_op jit(solution)/shard_map/ppermute | solution.py:150
  316.1 10.5 %collective-permute-done.13 = bf16[128,2048]{1,0:T(8,128)(2,1)} collective-permute-done((bf16[128,2048]{1,0:T(8,128)(2,1)S(1)}, bf16[128,2048]{1,0:T(8,128)(2,1)}, u32[]{:S(2)}, u32[]{:S(2)}) %collective-permute-start.13) | collective-permute-done | bytes 524320 | tf_op jit(solution)/shard_map/ppermute | solution.py:150
  326.7 10.6 %collective-permute-done.14 = bf16[128,2048]{1,0:T(8,128)(2,1)} collective-permute-done((bf16[128,2048]{1,0:T(8,128)(2,1)}, bf16[128,2048]{1,0:T(8,128)(2,1)}, u32[]{:S(2)}, u32[]{:S(2)}) %collective-permute-start.14) | collective-permute-done | bytes 524320 | tf_op jit(solution)/shard_map/ppermute | solution.py:150
  340.9 4.6 %fusion.2 = bf16[1024,2048]{1,0:T(8,128)(2,1)S(1)} fusion(s32[]{:T(128)S(6)} %select_n.80, bf16[1024,2048]{1,0:T(8,128)(2,1)S(1)} %constant_dynamic-update-slice_fusion.8), kind=kLoop, calls=%fused_computation.6 | loop fusion | flops 8388608 | bytes 8388612 | tf_op jit(solution)/shard_map/jit(_roll_dynamic)/concatenate | solution.py:153
  349.0 1.9 fusion.103
  351.9 1.7 fusion.24
  353.6 1.9 fusion.97
  357.3 2.1 add_convert_fusion
  359.8 2.5 convolution_convert_fusion.6
  364.1 2.1 add_convert_fusion.1
  366.3 28.4 %reduce-scatter.11.cloned.1.call-done = bf16[128,1024]{1,0:T(8,128)(2,1)} async-done(((bf16[1024,1024]{1,0:T(8,128)(2,1)}), bf16[128,1024]{1,0:T(8,128)(2,1)}) %reduce-scatter.11.cloned.1.call-update) | async-done | bytes 262160 | tf_op jit(solution)/shard_map/reduce_scatter | solution.py:190
  394.6 36.9 %reduce-scatter.9.cloned.1.call-done = bf16[128,1024]{1,0:T(8,128)(2,1)} async-done(((bf16[1024,1024]{1,0:T(8,128)(2,1)}), bf16[128,1024]{1,0:T(8,128)(2,1)}) %reduce-scatter.9.cloned.1.call-update) | async-done | bytes 262160 | tf_op jit(solution)/shard_map/reduce_scatter | solution.py:190
  432.7 2.1 maximum_bitcast_fusion
  (192 shorter events, 42.8 us)
Async XLA Ops:
  6.5 5.3 %copy-start = (bf16[1,2048,512]{2,1,0:T(8,128)(2,1)S(1)}, bf16[1,2048,512]{2,1,0:T(8,128)(2,1)}, u32[]{:S(2)}) copy-start(bf16[1,2048,512]{2,1,0:T(8,128)(2,1)} %param.30) | copy-start | bytes 6291460
  6.5 5.3 %copy-start.2 = (bf16[1,128,2048]{2,1,0:T(8,128)(2,1)S(1)}, bf16[1,128,2048]{2,1,0:T(8,128)(2,1)}, u32[]{:S(2)}) copy-start(bf16[1,128,2048]{2,1,0:T(8,128)(2,1)} %param.19) | copy-start | bytes 1572868
  6.5 5.3 %copy-start.23 = (f32[1,2048]{1,0:T(1,128)S(1)}, f32[1,2048]{1,0:T(1,128)}, u32[]{:S(2)}) copy-start(f32[1,2048]{1,0:T(1,128)} %param.25) | copy-start | bytes 24580
  6.5 182.1 %reduce-scatter.5.cloned.1.call-start = ((), (), s32[]{:S(2)}) async-start(), calls=%async_computation.4 | async-start | bytes 2359296 | tf_op jit(solution)/shard_map/reduce_scatter | solution.py:190
  8.6 5.0 %copy-start.15 = (bf16[2,1,1,768,512]{4,3,2,1,0:T(8,128)(2,1)S(1)}, bf16[2,1,1,768,512]{4,3,2,1,0:T(8,128)(2,1)}, u32[]{:S(2)}) copy-start(bf16[2,1,1,768,512]{4,3,2,1,0:T(8,128)(2,1)} %param.21) | copy-start | bytes 4718596
  11.9 3.1 copy-start.30
  11.9 4.9 %copy-start.26 = (f32[1,512]{1,0:T(1,128)S(1)}, f32[1,512]{1,0:T(1,128)}, u32[]{:S(2)}) copy-start(f32[1,512]{1,0:T(1,128)} %param.31) | copy-start | bytes 6148
  13.1 6.3 %copy-start.5 = (bf16[1,8,128,512]{3,2,1,0:T(8,128)(2,1)S(1)}, bf16[1,8,128,512]{3,2,1,0:T(8,128)(2,1)}, u32[]{:S(2)}) copy-start(bf16[1,8,128,512]{3,2,1,0:T(8,128)(2,1)} %param.27) | copy-start | bytes 3145732
  23.9 6.8 %copy-start.8 = (bf16[768,512]{1,0:T(8,128)(2,1)S(1)}, bf16[768,512]{1,0:T(8,128)(2,1)}, u32[]{:S(2)}) copy-start(bf16[768,512]{1,0:T(8,128)(2,1)} %get-tuple-element.11) | copy-start | bytes 2359300
  34.6 3.2 copy-start.21
  34.6 37.3 %copy-start.28 = (s32[2,1,128,6]{2,1,3,0:T(1,128)S(1)}, s32[2,1,128,6]{2,1,3,0:T(1,128)}, u32[]{:S(2)}) copy-start(s32[2,1,128,6]{2,1,3,0:T(1,128)} %param.23) | copy-start | bytes 18436
  34.6 37.3 %copy-start.29 = (f32[2,1,128,6]{2,1,3,0:T(1,128)S(1)}, f32[2,1,128,6]{2,1,3,0:T(1,128)}, u32[]{:S(2)}) copy-start(f32[2,1,128,6]{2,1,3,0:T(1,128)} %param.24) | copy-start | bytes 18436
  37.9 11.4 %collective-permute-start = (bf16[128,2048]{1,0:T(8,128)(2,1)S(1)}, bf16[128,2048]{1,0:T(8,128)(2,1)S(1)}, u32[]{:S(2)}, u32[]{:S(2)}) collective-permute-start(bf16[128,2048]{1,0:T(8,128)(2,1)S(1)} %multiply_convert_fusion.1), channel_id=1, source_target_pairs={{0,2},{2,4},{4,6},{6,8},{8,10},{10,12},{12,14},{14,0},{1,3},{3,5},... | collective-permute-start | bytes 1572872 | tf_op jit(solution)/shard_map/ppermute | solution.py:150
  50.2 10.4 %collective-permute-start.1 = (bf16[128,2048]{1,0:T(8,128)(2,1)S(1)}, bf16[128,2048]{1,0:T(8,128)(2,1)S(1)}, u32[]{:S(2)}, u32[]{:S(2)}) collective-permute-start(bf16[128,2048]{1,0:T(8,128)(2,1)S(1)} %collective-permute-done), channel_id=1, source_target_pairs={{0,2},{2,4},{4,6},{6,8},{8,10},{10,12},{12,14},{14,0},{1,3},{3,5},... | collective-permute-start | bytes 1572872 | tf_op jit(solution)/shard_map/ppermute | solution.py:150
  61.4 10.5 %collective-permute-start.2 = (bf16[128,2048]{1,0:T(8,128)(2,1)S(1)}, bf16[128,2048]{1,0:T(8,128)(2,1)}, u32[]{:S(2)}, u32[]{:S(2)}) collective-permute-start(bf16[128,2048]{1,0:T(8,128)(2,1)S(1)} %collective-permute-done.1), channel_id=1, source_target_pairs={{0,2},{2,4},{4,6},{6,8},{8,10},{10,12},{12,14},{14,0},{1,3},{3,5},... | collective-permute-start | bytes 1572872 | tf_op jit(solution)/shard_map/ppermute | solution.py:150
  71.9 17.2 %collective-permute-start.3 = (bf16[128,2048]{1,0:T(8,128)(2,1)}, bf16[128,2048]{1,0:T(8,128)(2,1)}, u32[]{:S(2)}, u32[]{:S(2)}) collective-permute-start(bf16[128,2048]{1,0:T(8,128)(2,1)} %collective-permute-done.2), channel_id=1, source_target_pairs={{0,2},{2,4},{4,6},{6,8},{8,10},{10,12},{12,14},{14,0},{1,3},{3,5},... | collective-permute-start | bytes 1572872 | tf_op jit(solution)/shard_map/ppermute | solution.py:150
  89.2 10.8 %collective-permute-start.4 = (bf16[128,2048]{1,0:T(8,128)(2,1)}, bf16[128,2048]{1,0:T(8,128)(2,1)}, u32[]{:S(2)}, u32[]{:S(2)}) collective-permute-start(bf16[128,2048]{1,0:T(8,128)(2,1)} %collective-permute-done.3), channel_id=1, source_target_pairs={{0,2},{2,4},{4,6},{6,8},{8,10},{10,12},{12,14},{14,0},{1,3},{3,5},... | collective-permute-start | bytes 1572872 | tf_op jit(solution)/shard_map/ppermute | solution.py:150
  99.9 10.7 %collective-permute-start.5 = (bf16[128,2048]{1,0:T(8,128)(2,1)}, bf16[128,2048]{1,0:T(8,128)(2,1)}, u32[]{:S(2)}, u32[]{:S(2)}) collective-permute-start(bf16[128,2048]{1,0:T(8,128)(2,1)} %collective-permute-done.4), channel_id=1, source_target_pairs={{0,2},{2,4},{4,6},{6,8},{8,10},{10,12},{12,14},{14,0},{1,3},{3,5},... | collective-permute-start | bytes 1572872 | tf_op jit(solution)/shard_map/ppermute | solution.py:150
  110.7 20.2 %collective-permute-start.6 = (bf16[128,2048]{1,0:T(8,128)(2,1)}, bf16[128,2048]{1,0:T(8,128)(2,1)S(1)}, u32[]{:S(2)}, u32[]{:S(2)}) collective-permute-start(bf16[128,2048]{1,0:T(8,128)(2,1)} %collective-permute-done.5), channel_id=1, source_target_pairs={{0,2},{2,4},{4,6},{6,8},{8,10},{10,12},{12,14},{14,0},{1,3},{3,5},... | collective-permute-start | bytes 1572872 | tf_op jit(solution)/shard_map/ppermute | solution.py:150
  123.9 22.9 %copy-start.9 = (bf16[704,2048]{1,0:T(8,128)(2,1)}, bf16[704,2048]{1,0:T(8,128)(2,1)S(1)}, u32[]{:S(2)}) copy-start(bf16[704,2048]{1,0:T(8,128)(2,1)S(1)} %get-tuple-element.9) | copy-start | bytes 8650756
  123.9 26.6 %copy-start.13 = (bf16[704,2048]{1,0:T(8,128)(2,1)}, bf16[704,2048]{1,0:T(8,128)(2,1)S(1)}, u32[]{:S(2)}) copy-start(bf16[704,2048]{1,0:T(8,128)(2,1)S(1)} %get-tuple-element.8) | copy-start | bytes 8650756
  123.9 11.3 %copy-start.19 = (bf16[128,2048]{1,0:T(8,128)(2,1)S(1)}, bf16[128,2048]{1,0:T(8,128)(2,1)}, u32[]{:S(2)}) copy-start(bf16[128,2048]{1,0:T(8,128)(2,1)} %copy-done.18) | copy-start | bytes 1572868
  124.0 11.3 %copy-start.17 = (bf16[128,2048]{1,0:T(8,128)(2,1)S(1)}, bf16[128,2048]{1,0:T(8,128)(2,1)}, u32[]{:S(2)}) copy-start(bf16[128,2048]{1,0:T(8,128)(2,1)} %copy-done.16) | copy-start | bytes 1572868
  135.5 5.9 %slice-start = ((s8[5767168]{0:T(1024)(128)(4,1)}), s8[4194304]{0:T(1024)(128)(4,1)S(1)}, s32[]{:S(2)}) async-start(s8[5767168]{0:T(1024)(128)(4,1)} %bitcast.318), calls=%async_computation.8 | async-start | bytes 8388608
  141.4 3.4 slice-start.4
  153.8 71.9 %reduce-scatter.7.cloned.1.call-start = ((), (), s32[]{:S(2)}) async-start(), calls=%async_computation.5 | async-start | bytes 2359296 | tf_op jit(solution)/shard_map/reduce_scatter | solution.py:190
  160.9 233.7 %reduce-scatter.11.cloned.1.call-start = ((), (), s32[]{:S(2)}) async-start(), calls=%async_computation.7 | async-start | bytes 2359296 | tf_op jit(solution)/shard_map/reduce_scatter | solution.py:190
  227.6 12.1 %collective-permute-start.7 = (bf16[128,2048]{1,0:T(8,128)(2,1)}, bf16[128,2048]{1,0:T(8,128)(2,1)S(1)}, u32[]{:S(2)}, u32[]{:S(2)}) collective-permute-start(bf16[128,2048]{1,0:T(8,128)(2,1)} %add_convert_fusion.5), channel_id=1, source_target_pairs={{0,1},{2,3},{4,5},{6,7},{8,9},{10,11},{12,13},{14,15},{16,17},{18,... | collective-permute-start | bytes 1572872 | tf_op jit(solution)/shard_map/ppermute | solution.py:14
  241.0 3.8 copy-start.3
  241.1 3.8 copy-start.27
  241.1 3.9 copy-start.6
  244.8 4.7 %copy-start.22 = (pred[128,896]{1,0:T(8,128)(4,1)S(1)}, pred[128,896]{1,0:T(8,128)(4,1)}, u32[]{:S(2)}) copy-start(pred[128,896]{1,0:T(8,128)(4,1)} %get-tuple-element.20) | copy-start | bytes 344068
  249.5 6.7 %copy-start.7 = (bf16[768,512]{1,0:T(8,128)(2,1)S(1)}, bf16[768,512]{1,0:T(8,128)(2,1)}, u32[]{:S(2)}) copy-start(bf16[768,512]{1,0:T(8,128)(2,1)} %get-tuple-element.10) | copy-start | bytes 2359300
  249.5 6.7 %copy-start.31 = (bf16[1,8,512,128]{3,2,1,0:T(8,128)(2,1)S(1)}, bf16[1,8,512,128]{3,2,1,0:T(8,128)(2,1)}, u32[]{:S(2)}) copy-start(bf16[1,8,512,128]{3,2,1,0:T(8,128)(2,1)} %param.28) | copy-start | bytes 3145732
  256.2 3.7 copy-start.4
  260.0 66.6 %copy-start.25 = (f32[8,1,64]{2,0,1:T(8,128)S(1)}, f32[8,1,64]{2,0,1:T(8,128)}, u32[]{:S(2)}) copy-start(f32[8,1,64]{2,0,1:T(8,128)} %get-tuple-element.16) | copy-start | bytes 6148
  260.0 66.7 %copy-start.24 = (f32[8,1,64]{2,0,1:T(8,128)S(1)}, f32[8,1,64]{2,0,1:T(8,128)}, u32[]{:S(2)}) copy-start(f32[8,1,64]{2,0,1:T(8,128)} %get-tuple-element.17) | copy-start | bytes 6148
  263.2 10.5 %collective-permute-start.8 = (bf16[128,2048]{1,0:T(8,128)(2,1)S(1)}, bf16[128,2048]{1,0:T(8,128)(2,1)S(1)}, u32[]{:S(2)}, u32[]{:S(2)}) collective-permute-start(bf16[128,2048]{1,0:T(8,128)(2,1)S(1)} %multiply_convert_fusion), channel_id=1, source_target_pairs={{0,2},{2,4},{4,6},{6,8},{8,10},{10,12},{12,14},{14,0},{1,3},{3,5},... | collective-permute-start | bytes 1572872 | tf_op jit(solution)/shard_map/ppermute | solution.py:150
  273.6 10.4 %collective-permute-start.9 = (bf16[128,2048]{1,0:T(8,128)(2,1)S(1)}, bf16[128,2048]{1,0:T(8,128)(2,1)S(1)}, u32[]{:S(2)}, u32[]{:S(2)}) collective-permute-start(bf16[128,2048]{1,0:T(8,128)(2,1)S(1)} %collective-permute-done.8), channel_id=1, source_target_pairs={{0,2},{2,4},{4,6},{6,8},{8,10},{10,12},{12,14},{14,0},{1,3},{3,5},... | collective-permute-start | bytes 1572872 | tf_op jit(solution)/shard_map/ppermute | solution.py:150
  284.0 10.4 %collective-permute-start.10 = (bf16[128,2048]{1,0:T(8,128)(2,1)S(1)}, bf16[128,2048]{1,0:T(8,128)(2,1)S(1)}, u32[]{:S(2)}, u32[]{:S(2)}) collective-permute-start(bf16[128,2048]{1,0:T(8,128)(2,1)S(1)} %collective-permute-done.9), channel_id=1, source_target_pairs={{0,2},{2,4},{4,6},{6,8},{8,10},{10,12},{12,14},{14,0},{1,3},{3,5},... | collective-permute-start | bytes 1572872 | tf_op jit(solution)/shard_map/ppermute | solution.py:150
  294.5 10.4 %collective-permute-start.11 = (bf16[128,2048]{1,0:T(8,128)(2,1)S(1)}, bf16[128,2048]{1,0:T(8,128)(2,1)S(1)}, u32[]{:S(2)}, u32[]{:S(2)}) collective-permute-start(bf16[128,2048]{1,0:T(8,128)(2,1)S(1)} %collective-permute-done.10), channel_id=1, source_target_pairs={{0,2},{2,4},{4,6},{6,8},{8,10},{10,12},{12,14},{14,0},{1,3},{3,5},... | collective-permute-start | bytes 1572872 | tf_op jit(solution)/shard_map/ppermute | solution.py:150
  304.9 10.4 %collective-permute-start.12 = (bf16[128,2048]{1,0:T(8,128)(2,1)S(1)}, bf16[128,2048]{1,0:T(8,128)(2,1)S(1)}, u32[]{:S(2)}, u32[]{:S(2)}) collective-permute-start(bf16[128,2048]{1,0:T(8,128)(2,1)S(1)} %collective-permute-done.11), channel_id=1, source_target_pairs={{0,2},{2,4},{4,6},{6,8},{8,10},{10,12},{12,14},{14,0},{1,3},{3,5},... | collective-permute-start | bytes 1572872 | tf_op jit(solution)/shard_map/ppermute | solution.py:150
  316.1 10.5 %collective-permute-start.13 = (bf16[128,2048]{1,0:T(8,128)(2,1)S(1)}, bf16[128,2048]{1,0:T(8,128)(2,1)}, u32[]{:S(2)}, u32[]{:S(2)}) collective-permute-start(bf16[128,2048]{1,0:T(8,128)(2,1)S(1)} %collective-permute-done.12), channel_id=1, source_target_pairs={{0,2},{2,4},{4,6},{6,8},{8,10},{10,12},{12,14},{14,0},{1,3},{3,5},... | collective-permute-start | bytes 1572872 | tf_op jit(solution)/shard_map/ppermute | solution.py:150
  326.6 10.7 %collective-permute-start.14 = (bf16[128,2048]{1,0:T(8,128)(2,1)}, bf16[128,2048]{1,0:T(8,128)(2,1)}, u32[]{:S(2)}, u32[]{:S(2)}) collective-permute-start(bf16[128,2048]{1,0:T(8,128)(2,1)} %collective-permute-done.13), channel_id=1, source_target_pairs={{0,2},{2,4},{4,6},{6,8},{8,10},{10,12},{12,14},{14,0},{1,3},{3,5},... | collective-permute-start | bytes 1572872 | tf_op jit(solution)/shard_map/ppermute | solution.py:150
  340.9 6.1 %slice-start.2 = ((s8[5767168]{0:T(1024)(128)(4,1)}), s8[4194304]{0:T(1024)(128)(4,1)S(1)}, s32[]{:S(2)}) async-start(s8[5767168]{0:T(1024)(128)(4,1)} %bitcast.320), calls=%async_computation.10 | async-start | bytes 8388608
  359.5 2.8 copy-start.37
  359.5 72.0 %reduce-scatter.9.cloned.1.call-start = ((), (), s32[]{:S(2)}) async-start(), calls=%async_computation.6 | async-start | bytes 2359296 | tf_op jit(solution)/shard_map/reduce_scatter | solution.py:190
  364.1 70.6 %copy-start.1 = (bf16[1,2048,512]{2,1,0:T(8,128)(2,1)S(1)}, bf16[1,2048,512]{2,1,0:T(8,128)(2,1)}, u32[]{:S(2)}) copy-start(bf16[1,2048,512]{2,1,0:T(8,128)(2,1)} %param.30) | copy-start | bytes 6291460
  (18 other events, 30.0 us)
Sparse Core Ops, SparseCore 0:
  153.9 34.6 reduce-scatter.4
  190.9 34.7 reduce-scatter.6
  359.6 34.9 reduce-scatter.10
  396.8 34.7 reduce-scatter.8
